TPU v7x, 256 devices: a whole 4x4x8 slice. The times are simulated.
256 devices in a mesh: pool: 4 (over x), section: 2 (over core), tensor: 32 (over z, y).
Axes of the slice: x: 4, y: 4, z: 8, core: 2. Of those that a mesh axis runs over, the one named last changes fastest.
Arguments:
- hidden_input: bfloat16 [2048, 8192], P('pool', 'tensor'), may hold values from -6 to 6
- attention_output: bfloat16 [2, 2048, 8192], P('section', 'pool', 'tensor'), may hold values from -6 to 6
- projection_weight: bfloat16 [2, 8192, 8192], P('section', 'tensor'), may hold values from -0.125 to 0.125
- lowrank_down_factor: bfloat16 [2, 128, 64, 8192], P('section', 'pool', None, 'tensor'), may hold values from -0.0625 to 0.0625
- lowrank_up_factor: bfloat16 [2, 128, 64, 8192], P('section', 'pool', None, 'tensor'), may hold values from -0.75 to 0.75
- residual_block_mats: bfloat16 [2, 128, 32, 128, 128], P('section', 'pool', 'tensor'), may hold values from -0.5 to 0.5
- diagonal_block_index: int32 [2, 128, 32], P('section', 'pool', 'tensor'), may hold values from 0 to 63, as said below
- row_variant_index: int32 [2048], P('pool'), may hold values from 0 to 127, as said below
Outputs:
- hidden_out: bfloat16 [2, 2048, 8192], P('section', 'pool', 'tensor')
Inputs may be any that keep to these rules, and one draw needn't show every extreme that they name: `row_variant_index`: within each aligned block of 512 rows the ids never fall; at most 256 rows of a block name variants of one owner q (ids q * 32 to (q + 1) * 32 - 1), and some owner receives exactly 256 rows from every block. `diagonal_block_index`: entry j of each list lies in j * 2 to (j + 1) * 2 - 1.
All inputs are finite; a program needn't handle non-finite values.
Results may differ from a plain program's by a relative error of at most 0.017.
Values may be sent and summed in bfloat16 or wider, within the bound.
No kernel may reach another device: no remote copies, remote signals or barrier semaphores. Data moves between devices by JAX's collectives and lax.ppermute only.
A program may use at most 128 MiB of HBM per device.

v0:
```python
import jax
import jax.numpy as jnp
from jax import lax
from jax.sharding import Mesh
from jax.sharding import PartitionSpec as P

TENSOR = ("tensor_0", "tensor_1")


def summed_rows(terms, axes):
    total = terms.astype(jnp.bfloat16)
    for axis in axes:
        total = lax.psum_scatter(total, axis, scatter_dimension=0, tiled=True)
    return total.astype(jnp.float32)


def rows_for(lines, peers):
    spare = -lines.shape[0] % peers
    if not spare:
        return lines
    return jnp.concatenate([lines, jnp.zeros((spare, *lines.shape[1:]), lines.dtype)])


def sent_to_all(x, axis):
    peers = lax.axis_size(axis)
    return lax.all_to_all(jnp.broadcast_to(x[None], (peers, *x.shape)), axis, 0, 0, tiled=True)


def joined_along(parts, dim):
    dims = list(parts.shape[1:])
    dims[dim] *= parts.shape[0]
    return jnp.moveaxis(parts, 0, dim).reshape(dims)


def gather_directly(x, axis, dim):
    parts = sent_to_all(x, axis)
    return joined_along(parts, dim)


def in_blocks(x, dim, peers):
    before, after = (x.shape[:dim], x.shape[dim + 1 :])
    return jnp.moveaxis(x.reshape(*before, peers, -1, *after), dim, 0)


def summed_on_arrival(x, axis, dim):
    parts = in_blocks(x, dim, lax.axis_size(axis))
    arrived = lax.all_to_all(parts, axis, split_axis=0, concat_axis=0, tiled=True)
    return arrived.astype(jnp.float32).sum(axis=0)


def total_of(x, axes):
    lines = x.reshape(-1, x.shape[-1])
    padded = rows_for(lines, lax.axis_size(axes))
    whole = gather_directly(summed_on_arrival(padded, axes, 0).astype(jnp.bfloat16), axes, 0)
    return lax.slice_in_dim(whole, 0, len(lines)).reshape(x.shape).astype(jnp.float32)


def shifted(value, axis, steps):
    count = lax.axis_size(axis)
    first, last = (max(0, -steps), min(count, count - steps))
    return lax.ppermute(value, axis, [(source, source + steps) for source in range(first, last)])


def adapter_delta(
    features, select, down_factor_rows, up_factor_rows, block_mats, place_hot, reducer
):
    var_count, low_dim, shard_width = down_factor_rows.shape
    block_size = block_mats.shape[-1]
    per_shard = shard_width // block_size
    projected = lax.dot_general(
        features,
        down_factor_rows.reshape(var_count * low_dim, shard_width),
        (((1,), (1,)), ((), ())),
        preferred_element_type=jnp.float32,
    )
    partial_value = jnp.einsum("svr,sv->sr", projected.reshape(-1, var_count, low_dim), select)
    lowrank_product = reducer(partial_value).astype(jnp.bfloat16)
    spread = (select.astype(jnp.bfloat16)[:, :, None] * lowrank_product[:, None, :]).reshape(
        -1, var_count * low_dim
    )
    lowrank_output = jnp.dot(
        spread,
        up_factor_rows.reshape(var_count * low_dim, shard_width),
        preferred_element_type=jnp.float32,
    )
    row_place = jnp.dot(select, place_hot.astype(jnp.float32))
    feat_blocks = features.reshape(-1, per_shard, block_size)
    picked = jnp.sum(feat_blocks * row_place.astype(jnp.bfloat16)[:, :, None], axis=1)
    stacked = jnp.transpose(block_mats, (1, 0, 2)).reshape(block_size, var_count * block_size)
    block_y = jnp.dot(picked, stacked, preferred_element_type=jnp.float32).reshape(
        -1, var_count, block_size
    )
    block_sel = jnp.einsum("svj,sv->sj", block_y, select)
    block_output = (row_place[:, :, None] * block_sel[:, None, :]).reshape(-1, shard_width)
    return (lowrank_output + block_output).astype(jnp.bfloat16)


def per_device(
    hidden_input,
    attention_output,
    projection_weight,
    lowrank_down_factor,
    lowrank_up_factor,
    residual_block_mats,
    diagonal_block_index,
    row_variant_index,
):
    features = attention_output[0]
    weight = projection_weight[0]
    row_count_dev, shard_width = features.shape
    down_factor_rows = lowrank_down_factor[0]
    up_factor_rows = lowrank_up_factor[0]
    block_mats = residual_block_mats[0][:, 0]
    var_count = down_factor_rows.shape[0]
    block_size = block_mats.shape[-1]
    per_shard = shard_width // block_size
    tensor_pos = lax.axis_index(TENSOR)
    section_pos = lax.axis_index("section")
    place_hot = (
        (diagonal_block_index[0][:, 0] - tensor_pos * per_shard)[:, None]
        == jnp.arange(per_shard)[None, :]
    ).astype(jnp.bfloat16)
    base_sum = summed_rows(
        lax.dot_general(
            weight, features, (((0,), (1,)), ((), ())), preferred_element_type=jnp.float32
        ),
        TENSOR,
    )
    pool_count = lax.axis_size("pool")
    capacity = row_count_dev // 2
    owners = row_variant_index // var_count
    owner_hot = (owners[:, None] == jnp.arange(pool_count)[None, :]).astype(jnp.int32)
    counts = jnp.sum(owner_hot, axis=0)
    starts = jnp.cumsum(counts) - counts
    slot_pos = jnp.arange(row_count_dev) - jnp.sum(owner_hot * starts[None, :], axis=1)
    filled = jnp.arange(capacity)[None, :] < counts[:, None]
    source = jnp.minimum(starts[:, None] + jnp.arange(capacity)[None, :], row_count_dev - 1)
    send_feat = jnp.where(
        filled[:, :, None], jnp.take(features, source, axis=0), jnp.zeros((), jnp.bfloat16)
    )
    send_var = jnp.where(
        filled,
        jnp.take(row_variant_index, source) - jnp.arange(pool_count)[:, None] * var_count,
        -1,
    ).astype(jnp.bfloat16)
    recv_feat = lax.all_to_all(send_feat, "pool", split_axis=0, concat_axis=0, tiled=True)
    recv_var = lax.all_to_all(send_var, "pool", split_axis=0, concat_axis=0, tiled=True)
    group_count, item_count = recv_var.shape
    flat_var = recv_var.reshape(group_count * item_count)
    select = (flat_var[:, None] == jnp.arange(var_count).astype(jnp.bfloat16)[None, :]).astype(
        jnp.float32
    )

    def slot_reduce(partial_value):
        return total_of(partial_value.astype(jnp.bfloat16), TENSOR)

    served = adapter_delta(
        recv_feat.reshape(group_count * item_count, shard_width),
        select,
        down_factor_rows,
        up_factor_rows,
        block_mats,
        place_hot,
        slot_reduce,
    )
    returned = lax.all_to_all(
        served.reshape(group_count, item_count, shard_width),
        "pool",
        split_axis=0,
        concat_axis=0,
        tiled=True,
    )
    flat_back = returned.reshape(pool_count * capacity, shard_width)
    adapter_output = jnp.take(flat_back, owners * capacity + slot_pos, axis=0)
    branch = jnp.transpose(base_sum) + adapter_output.astype(jnp.float32)
    first_out = (hidden_input.astype(jnp.float32) + branch).astype(jnp.bfloat16)
    carried = shifted(first_out, "section", 1)
    start_rows = jnp.where(section_pos == 0, hidden_input, carried)
    return (start_rows.astype(jnp.float32) + branch).astype(jnp.bfloat16)[None]


def solution(mesh):
    finer = Mesh(
        mesh.devices.reshape(mesh.shape["pool"], mesh.shape["section"], 8, 4),
        ("pool", "section", "tensor_0", "tensor_1"),
    )
    placed = (
        P("pool", TENSOR),
        P("section", "pool", TENSOR),
        P("section", TENSOR, None),
        P("section", "pool", None, TENSOR),
        P("section", "pool", None, TENSOR),
        P("section", "pool", TENSOR, None, None),
        P("section", "pool", TENSOR),
        P("pool"),
    )
    return jax.shard_map(
        per_device,
        mesh=finer,
        in_specs=placed,
        out_specs=P("section", "pool", TENSOR),
        check_vma=False,
    )
```

profile of v0, /device:TPU:1, one launch (start us, length us, event | category | flops | bytes accessed | tf_op | source)
XLA Modules:
  0.0 174.7 jit_solution(16107897178203949886)
XLA Ops:
  6.5 7.9 %convolution_convert_fusion = bf16[8192,512]{1,0:T(8,128)(2,1)} fusion(bf16[1,256,8192]{2,1,0:T(8,128)(2,1)} %param.10, bf16[1,512,256]{2,1,0:T(8,128)(2,1)} %param.9), kind=kOutput, calls=%fused_computation.5 | convolution fusion | flops 2151677952 | bytes 12845056 | tf_op jit(solution)/shard_map/dot_general | solution.py:124
  14.9 6.9 %gather_fusion = s32[1024]{0:T(1024)S(1)} fusion(s32[512]{0:T(512)S(1)} %copy-done.1, s32[1024]{0:T(1024)S(1)} %broadcast_clamp_fusion), kind=kCustom, calls=%fused_computation | custom fusion | bytes 12288 | tf_op jit(solution)/shard_map/jit(_take)/gather | solution.py:143
  22.4 0.7 reduce.5
  23.7 4.8 %all-to-all-start = ((bf16[4,2,128]{2,1,0:T(2,128)(2,1)}), bf16[4,2,128]{2,1,0:T(2,128)(2,1)S(1)}, u32[]{:S(2)}, u32[]{:S(2)}) async-start(bf16[4,2,128]{2,1,0:T(2,128)(2,1)} %reshape.358), calls=%async_computation.2 | async-start | bytes 4096 | tf_op jit(solution)/shard_map/all_to_all | solution.py:147
  28.5 3.9 %gather_fusion.1 = bf16[1024,256]{1,0:T(8,128)(2,1)S(1)} fusion(bf16[512,256]{1,0:T(8,128)(2,1)S(1)} %bitcast.67, s32[1024]{0:T(1024)S(1)} %broadcast_clamp_fusion), kind=kCustom, calls=%fused_computation.1 | custom fusion | bytes 1052672 | tf_op jit(solution)/shard_map/jit(_take)/gather | solution.py:139
  32.6 1.2 select_select_fusion
  34.5 4.2 %all-to-all-start.1 = ((bf16[4,256,256]{2,1,0:T(8,128)(2,1)}), bf16[4,256,256]{2,1,0:T(8,128)(2,1)S(1)}, u32[]{:S(2)}, u32[]{:S(2)}) async-start(bf16[4,256,256]{2,1,0:T(8,128)(2,1)} %select_select_fusion), calls=%async_computation.3 | async-start | bytes 1048576 | tf_op jit(solution)/shard_map/all_to_all | solution.py:146
  39.3 0.7 compare_bitcast_fusion
  40.0 1.5 copy.52
  41.5 1.1 copy.40
  42.5 3.4 %all-to-all-done.1 = bf16[4,256,256]{2,1,0:T(8,128)(2,1)S(1)} async-done(((bf16[4,256,256]{2,1,0:T(8,128)(2,1)}), bf16[4,256,256]{2,1,0:T(8,128)(2,1)S(1)}, u32[]{:S(2)}, u32[]{:S(2)}) %all-to-all-start.1) | async-done | bytes 524320 | tf_op jit(solution)/shard_map/all_to_all | solution.py:146
  45.9 2.5 %multiply_reduce_fusion = bf16[1024,64]{0,1:T(8,128)(2,1)S(1)} fusion(f32[1024,32]{0,1:T(8,128)S(1)} %get-tuple-element.9, bf16[1024,256,1]{1,0,2:T(8,128)(2,1)S(1)} %bitcast.70, bf16[1,32,64,256]{3,2,1,0:T(8,128)(2,1)} %param.11), kind=kOutput, calls=%fused_computation.6 | convolution fusion | flops 1077870592 | bytes 1835008 | tf_op jit(solution)/shard_map/dot_general | solution.py:70
  48.6 0.9 reshape.360
  49.5 11.8 %all-to-all-start.2 = ((bf16[32,2,1024]{2,1,0:T(2,128)(2,1)}), bf16[32,2,1024]{2,1,0:T(2,128)(2,1)S(1)}, u32[]{:S(2)}, u32[]{:S(2)}) async-start(bf16[32,2,1024]{2,1,0:T(2,128)(2,1)} %reshape.360), calls=%async_computation.4 | async-start | bytes 262144 | tf_op jit(solution)/shard_map/all_to_all | solution.py:47
  61.6 5.7 %multiply_reduce_fusion.1 = bf16[1024,128]{1,0:T(8,128)(2,1)S(1)} fusion(bf16[1024,2,128]{2,1,0:T(2,128)(2,1)S(1)} %reshape_reshape.3, bf16[1024,2]{1,0:T(8,128)(2,1)S(1)} %copy.41), kind=kLoop, calls=%fused_computation.18 | loop fusion | flops 393216 | bytes 790528 | tf_op jit(solution)/shard_map/reduce_sum | solution.py:88
  67.3 5.6 %fusion.4 = bf16[1024,32,128]{2,0,1:T(8,128)(2,1)} fusion(bf16[1,32,1,128,128]{3,4,1,2,0:T(8,128)(2,1)S(1)} %copy.42, bf16[1024,128]{1,0:T(8,128)(2,1)S(1)} %multiply_reduce_fusion.1), kind=kOutput, calls=%fused_computation.11 | convolution fusion | flops 1073741824 | bytes 9699328 | tf_op jit(solution)/shard_map/dot_general | solution.py:90
  72.9 43.2 %reduce-scatter.3.cloned.1.call-done = bf16[1024,512]{1,0:T(8,128)(2,1)} async-done(((bf16[8192,512]{1,0:T(8,128)(2,1)}), bf16[1024,512]{1,0:T(8,128)(2,1)}) %reduce-scatter.3.cloned.1.call-update) | async-done | bytes 1048592 | tf_op jit(solution)/shard_map/reduce_scatter | solution.py:13
  116.2 8.6 %fusion = f32[1024,1,128]{2,1,0:T(1,128)S(1)} fusion(pred[1024,32,1]{1,2,0:T(4,128)(4,1)S(1)} %copy-done.5, bf16[1024,32,128]{2,0,1:T(8,128)(2,1)} %fusion.4), kind=kOutput, calls=%fused_computation.3 | convolution fusion | flops 8388608 | bytes 8945664 | tf_op jit(solution)/shard_map/svj,sv->sj/dot_general | solution.py:93
  125.2 0.8 reshape.362
  126.0 7.1 %all-to-all-start.3 = ((bf16[32,2,1024]{2,1,0:T(2,128)(2,1)}), bf16[32,2,1024]{2,1,0:T(2,128)(2,1)S(1)}, u32[]{:S(2)}, u32[]{:S(2)}) async-start(bf16[32,2,1024]{2,1,0:T(2,128)(2,1)} %reshape.362), calls=%async_computation.5 | async-start | bytes 262144 | tf_op jit(solution)/shard_map/all_to_all | solution.py:26
  133.2 3.9 %broadcast_multiply_fusion.1 = f32[1024,2,128]{2,1,0:T(2,128)S(1)} fusion(f32[1024,128]{1,0:T(8,128)S(1)} %bitcast.75, f32[1024,2]{1,0:T(8,128)S(1)} %copy-done.3), kind=kLoop, calls=%fused_computation.17 | loop fusion | flops 262144 | bytes 1581056 | tf_op jit(solution)/shard_map/mul | solution.py:94
  137.1 5.2 %all-to-all-done.3 = bf16[32,2,1024]{2,1,0:T(2,128)(2,1)S(1)} async-done(((bf16[32,2,1024]{2,1,0:T(2,128)(2,1)}), bf16[32,2,1024]{2,1,0:T(2,128)(2,1)S(1)}, u32[]{:S(2)}, u32[]{:S(2)}) %all-to-all-start.3) | async-done | bytes 131104 | tf_op jit(solution)/shard_map/all_to_all | solution.py:26
  142.7 1.1 broadcast_multiply_fusion
  143.8 2.1 %fusion.3 = bf16[1024,256]{1,0:T(8,128)(2,1)} fusion(bf16[1024,2048]{0,1:T(8,128)(2,1)S(1)} %bitcast.69, bf16[2048,256]{1,0:T(8,128)(2,1)S(1)} %bitcast.66, f32[128,8,2,128]{3,2,1,0:T(2,128)S(1)} %bitcast.74), kind=kOutput, calls=%fused_computation.10 | convolution fusion | flops 1074266112 | bytes 6815744 | tf_op jit(solution)/shard_map/dot_general | solution.py:81
  145.9 4.0 %all-to-all-start.4 = ((bf16[4,256,256]{2,1,0:T(8,128)(2,1)}), bf16[4,256,256]{2,1,0:T(8,128)(2,1)S(1)}, u32[]{:S(2)}, u32[]{:S(2)}) async-start(bf16[4,256,256]{2,1,0:T(8,128)(2,1)} %bitcast.24), calls=%async_computation.6 | async-start | bytes 1048576 | tf_op jit(solution)/shard_map/all_to_all | solution.py:166
  150.1 6.7 %all-to-all-done.4 = bf16[4,256,256]{2,1,0:T(8,128)(2,1)S(1)} async-done(((bf16[4,256,256]{2,1,0:T(8,128)(2,1)}), bf16[4,256,256]{2,1,0:T(8,128)(2,1)S(1)}, u32[]{:S(2)}, u32[]{:S(2)}) %all-to-all-start.4) | async-done | bytes 524320 | tf_op jit(solution)/shard_map/all_to_all | solution.py:166
  156.8 1.9 %gather_fusion.2 = bf16[512,256]{1,0:T(8,128)(2,1)S(1)} fusion(bf16[1024,256]{1,0:T(8,128)(2,1)S(1)} %bitcast.68, s32[1024]{0:T(1024)S(1)} %pad_clamp_fusion), kind=kCustom, calls=%fused_computation.2 | custom fusion | bytes 526336 | tf_op jit(solution)/shard_map/jit(_take)/gather | solution.py:174
  159.0 1.1 add_convert_fusion.1
  160.1 1.3 collective-permute-start
  161.4 4.6 %collective-permute-done = bf16[512,256]{0,1:T(8,128)(2,1)S(1)} collective-permute-done((bf16[512,256]{0,1:T(8,128)(2,1)S(1)}, bf16[512,256]{0,1:T(8,128)(2,1)S(1)}, u32[]{:S(2)}, u32[]{:S(2)}) %collective-permute-start) | collective-permute-done | bytes 262176 | tf_op jit(solution)/shard_map/ppermute | solution.py:61
  165.9 1.1 fusion.7
  167.1 0.8 copy.45
  (55 shorter events, 4.6 us)
Async XLA Ops:
  6.5 137.3 %copy-start = (bf16[1,32,64,256]{3,2,1,0:T(8,128)(2,1)S(1)}, bf16[1,32,64,256]{3,2,1,0:T(8,128)(2,1)}, u32[]{:S(2)}) copy-start(bf16[1,32,64,256]{3,2,1,0:T(8,128)(2,1)} %param.12) | copy-start | bytes 3145732
  6.5 8.0 %copy-start.1 = (s32[512]{0:T(512)S(1)}, s32[512]{0:T(512)}, u32[]{:S(2)}) copy-start(s32[512]{0:T(512)} %param.15) | copy-start | bytes 6148
  6.5 109.6 %reduce-scatter.3.cloned.1.call-start = ((), (), s32[]{:S(2)}) async-start(), calls=%async_computation.7 | async-start | bytes 9437184 | tf_op jit(solution)/shard_map/reduce_scatter | solution.py:13
  14.5 14.0 %copy-start.2 = (bf16[1,512,256]{2,1,0:T(8,128)(2,1)S(1)}, bf16[1,512,256]{2,1,0:T(8,128)(2,1)}, u32[]{:S(2)}) copy-start(bf16[1,512,256]{2,1,0:T(8,128)(2,1)} %param.9) | copy-start | bytes 786436
  14.5 18.0 %copy-start.7 = (s32[1,32,1]{1,2,0:T(1,128)S(1)}, s32[1,32,1]{1,2,0:T(1,128)}, u32[]{:S(2)}) copy-start(s32[1,32,1]{1,2,0:T(1,128)} %param.14) | copy-start | bytes 388
  14.5 19.3 %copy-start.4 = (bf16[1,32,1,128,128]{4,3,2,1,0:T(8,128)(2,1)S(1)}, bf16[1,32,1,128,128]{4,3,2,1,0:T(8,128)(2,1)}, u32[]{:S(2)}) copy-start(bf16[1,32,1,128,128]{4,3,2,1,0:T(8,128)(2,1)} %param.13) | copy-start | bytes 3145732
  23.7 10.8 %all-to-all-start = ((bf16[4,2,128]{2,1,0:T(2,128)(2,1)}), bf16[4,2,128]{2,1,0:T(2,128)(2,1)S(1)}, u32[]{:S(2)}, u32[]{:S(2)}) async-start(bf16[4,2,128]{2,1,0:T(2,128)(2,1)} %reshape.358), calls=%async_computation.2 | async-start | bytes 4096 | tf_op jit(solution)/shard_map/all_to_all | solution.py:147
  34.5 11.4 %all-to-all-start.1 = ((bf16[4,256,256]{2,1,0:T(8,128)(2,1)}), bf16[4,256,256]{2,1,0:T(8,128)(2,1)S(1)}, u32[]{:S(2)}, u32[]{:S(2)}) async-start(bf16[4,256,256]{2,1,0:T(8,128)(2,1)} %select_select_fusion), calls=%async_computation.3 | async-start | bytes 1048576 | tf_op jit(solution)/shard_map/all_to_all | solution.py:146
  49.5 75.3 %all-to-all-start.2 = ((bf16[32,2,1024]{2,1,0:T(2,128)(2,1)}), bf16[32,2,1024]{2,1,0:T(2,128)(2,1)S(1)}, u32[]{:S(2)}, u32[]{:S(2)}) async-start(bf16[32,2,1024]{2,1,0:T(2,128)(2,1)} %reshape.360), calls=%async_computation.4 | async-start | bytes 262144 | tf_op jit(solution)/shard_map/all_to_all | solution.py:47
  61.3 97.7 %reduce-scatter.5.cloned.1.call-start = ((), (), s32[]{:S(2)}) async-start(), calls=%async_computation.8 | async-start | bytes 1310720 | tf_op jit(solution)/shard_map/reduce_scatter | solution.py:13
  67.3 48.8 %copy-start.5 = (pred[1024,32,1]{1,2,0:T(4,128)(4,1)S(1)}, pred[1024,32,1]{1,2,0:T(4,128)(4,1)}, u32[]{:S(2)}) copy-start(pred[1024,32,1]{1,2,0:T(4,128)(4,1)} %copy.52) | copy-start | bytes 98308
  72.9 60.3 %copy-start.3 = (f32[1024,2]{1,0:T(8,128)S(1)}, f32[1024,2]{1,0:T(8,128)}, u32[]{:S(2)}) copy-start(f32[1024,2]{1,0:T(8,128)} %copy.40) | copy-start | bytes 24580
  126.0 16.3 %all-to-all-start.3 = ((bf16[32,2,1024]{2,1,0:T(2,128)(2,1)}), bf16[32,2,1024]{2,1,0:T(2,128)(2,1)S(1)}, u32[]{:S(2)}, u32[]{:S(2)}) async-start(bf16[32,2,1024]{2,1,0:T(2,128)(2,1)} %reshape.362), calls=%async_computation.5 | async-start | bytes 262144 | tf_op jit(solution)/shard_map/all_to_all | solution.py:26
  142.5 7.4 %copy-start.6 = (bf16[512,256]{1,0:T(8,128)(2,1)S(1)}, bf16[512,256]{1,0:T(8,128)(2,1)}, u32[]{:S(2)}) copy-start(bf16[512,256]{1,0:T(8,128)(2,1)} %param.8) | copy-start | bytes 786436
  145.9 10.9 %all-to-all-start.4 = ((bf16[4,256,256]{2,1,0:T(8,128)(2,1)}), bf16[4,256,256]{2,1,0:T(8,128)(2,1)S(1)}, u32[]{:S(2)}, u32[]{:S(2)}) async-start(bf16[4,256,256]{2,1,0:T(8,128)(2,1)} %bitcast.24), calls=%async_computation.6 | async-start | bytes 1048576 | tf_op jit(solution)/shard_map/all_to_all | solution.py:166
  160.1 5.9 %collective-permute-start = (bf16[512,256]{0,1:T(8,128)(2,1)S(1)}, bf16[512,256]{0,1:T(8,128)(2,1)S(1)}, u32[]{:S(2)}, u32[]{:S(2)}) collective-permute-start(bf16[512,256]{0,1:T(8,128)(2,1)S(1)} %add_convert_fusion.1), channel_id=1, source_target_pairs={{0,32},{1,33},{2,34},{3,35},{4,36},{5,37},{6,38},{7,39},{8,40},{9,... | collective-permute-start | bytes 786440 | tf_op jit(solution)/shard_map/ppermute | solution.py:61
Sparse Core Ops, SparseCore 0:
  14.6 101.4 reduce-scatter.2
  118.7 24.1 reduce-scatter.4
where the time goes:
time: 175 us
  waiting for transfers between devices  63.1 us (36%)
  starting transfers between devices  33.5 us (19%)
  matrix products  27 us (15%)
  local copies, waits for them, and re-layouts  21.1 us (12%)
  other arithmetic  16.3 us (9%)
  between operations  13.7 us (8%)
    reduce_scatter x2, waiting for transfers between devices, summed_rows(): total = lax.psum_scatter(total, axis, scatter_dimension=0, tiled=True)  43.3 us
    all_to_all x1, starting transfers between devices, summed_on_arrival(): lax.all_to_all(parts, axis, split_axis=0, concat_axis=0, tiled=True)  11.8 us
    dot_general x1, matrix products, adapter_delta(): block_sel = jnp.einsum('svj,sv->sj', block_y, select)  8.65 us
    dot_general x1, matrix products, per_device(): lax.dot_general(weight, features, (((0,), (1,)), ((), ())), preferred_ele...  7.94 us
    all_to_all x1, starting transfers between devices, sent_to_all(): lax.all_to_all(jnp.broadcast_to(x[None], (peers, *x.shape)), axis, 0, 0,...  7.14 us
    gather x1, local copies, waits for them, and re-layouts, per_device(): jnp.take(row_variant_index, source)  6.86 us
    all_to_all x1, waiting for transfers between devices, per_device(): lax.all_to_all(served.reshape(group_count, item_count, shard_width), 'poo...  6.68 us
    reduce_sum x1, other arithmetic, adapter_delta(): jnp.sum(feat_blocks * row_place.astype(jnp.bfloat16)[:, :, None], axis=1)  5.66 us
  transfers between devices with their start and end apart: 8, of which 5 were waited for; matrix products, arithmetic and copies ran while one was open for 31% of the time, Pallas kernels for 0%

commit v1 on v0

--- a/solution.py
+++ b/solution.py
@@ -9,8 +9,7 @@
 
 def summed_rows(terms, axes):
     total = terms.astype(jnp.bfloat16)
-    for axis in axes:
-        total = lax.psum_scatter(total, axis, scatter_dimension=0, tiled=True)
+    total = lax.psum_scatter(total, axes, scatter_dimension=0, tiled=True)
     return total.astype(jnp.float32)
 
 

time: 175 us -> 264 us (1.51)
  waiting for transfers between devices: 63.1 us -> 145 us
  matrix products: 27 us -> 32.9 us
    reduce_scatter x2 -> x1, waiting for transfers between devices: 43.3 us -> 123 us  [summed_rows(): total = lax.psum_scatter(total, axes, scatter_dimension=0, tiled=True)]
    dot_general x1, matrix products: 8.65 us -> 17.7 us  [adapter_delta(): block_sel = jnp.einsum('svj,sv->sj', block_y, select)]
    dot_general x1, matrix products: 5.56 us -> 2.35 us  [adapter_delta(): jnp.dot(picked, stacked, preferred_element_type=jnp.float32)]
  transfers between devices with their start and end apart: 8 -> 7, of which waited for: 5 -> 5; matrix products, arithmetic and copies ran while one was open for 31% -> 22% of each run, Pallas kernels for 0% -> 0%
where the time goes in v1:
time: 264 us
  waiting for transfers between devices  145 us (55%)
  starting transfers between devices  35.1 us (13%)
  matrix products  32.9 us (12%)
  local copies, waits for them, and re-layouts  21.1 us (8%)
  other arithmetic  16.3 us (6%)
  between operations  13.7 us (5%)
    reduce_scatter x1, waiting for transfers between devices, summed_rows(): total = lax.psum_scatter(total, axes, scatter_dimension=0, tiled=True)  123 us
    dot_general x1, matrix products, adapter_delta(): block_sel = jnp.einsum('svj,sv->sj', block_y, select)  17.7 us
    all_to_all x1, starting transfers between devices, summed_on_arrival(): lax.all_to_all(parts, axis, split_axis=0, concat_axis=0, tiled=True)  11.8 us
    all_to_all x1, starting transfers between devices, sent_to_all(): lax.all_to_all(jnp.broadcast_to(x[None], (peers, *x.shape)), axis, 0, 0,...  9.44 us
    dot_general x1, matrix products, per_device(): lax.dot_general(weight, features, (((0,), (1,)), ((), ())), preferred_ele...  7.94 us
    gather x1, local copies, waits for them, and re-layouts, per_device(): jnp.take(row_variant_index, source)  6.86 us
    all_to_all x1, waiting for transfers between devices, per_device(): lax.all_to_all(served.reshape(group_count, item_count, shard_width), 'poo...  6.63 us
    all_to_all x1, waiting for transfers between devices, sent_to_all(): lax.all_to_all(jnp.broadcast_to(x[None], (peers, *x.shape)), axis, 0, 0,...  6.3 us
  transfers between devices with their start and end apart: 7, of which 5 were waited for; matrix products, arithmetic and copies ran while one was open for 22% of the time, Pallas kernels for 0%

profile of v1, /device:TPU:1, one launch (start us, length us, event | category | flops | bytes accessed | tf_op | source)
XLA Modules:
  0.0 263.7 jit_solution(18358166597891135268)
XLA Ops:
  6.5 7.9 %convolution_convert_fusion = bf16[8192,512]{1,0:T(8,128)(2,1)} fusion(bf16[1,256,8192]{2,1,0:T(8,128)(2,1)} %param.10, bf16[1,512,256]{2,1,0:T(8,128)(2,1)} %param.9), kind=kOutput, calls=%fused_computation.5 | convolution fusion | flops 2151677952 | bytes 12845056 | tf_op jit(solution)/shard_map/dot_general | solution.py:123
  14.9 6.9 %gather_fusion = s32[1024]{0:T(1024)S(1)} fusion(s32[512]{0:T(512)S(1)} %copy-done.1, s32[1024]{0:T(1024)S(1)} %broadcast_clamp_fusion), kind=kCustom, calls=%fused_computation | custom fusion | bytes 12288 | tf_op jit(solution)/shard_map/jit(_take)/gather | solution.py:142
  22.4 0.7 reduce.5
  23.7 4.8 %all-to-all-start = ((bf16[4,2,128]{2,1,0:T(2,128)(2,1)}), bf16[4,2,128]{2,1,0:T(2,128)(2,1)S(1)}, u32[]{:S(2)}, u32[]{:S(2)}) async-start(bf16[4,2,128]{2,1,0:T(2,128)(2,1)} %reshape.358), calls=%async_computation.1 | async-start | bytes 4096 | tf_op jit(solution)/shard_map/all_to_all | solution.py:146
  28.5 3.9 %gather_fusion.1 = bf16[1024,256]{1,0:T(8,128)(2,1)S(1)} fusion(bf16[512,256]{1,0:T(8,128)(2,1)S(1)} %bitcast.67, s32[1024]{0:T(1024)S(1)} %broadcast_clamp_fusion), kind=kCustom, calls=%fused_computation.1 | custom fusion | bytes 1052672 | tf_op jit(solution)/shard_map/jit(_take)/gather | solution.py:138
  32.6 1.2 select_select_fusion
  34.5 4.2 %all-to-all-start.1 = ((bf16[4,256,256]{2,1,0:T(8,128)(2,1)}), bf16[4,256,256]{2,1,0:T(8,128)(2,1)S(1)}, u32[]{:S(2)}, u32[]{:S(2)}) async-start(bf16[4,256,256]{2,1,0:T(8,128)(2,1)} %select_select_fusion), calls=%async_computation.2 | async-start | bytes 1048576 | tf_op jit(solution)/shard_map/all_to_all | solution.py:145
  39.3 0.7 compare_bitcast_fusion
  40.0 1.5 copy.52
  41.5 1.0 copy.40
  42.5 3.4 %all-to-all-done.1 = bf16[4,256,256]{2,1,0:T(8,128)(2,1)S(1)} async-done(((bf16[4,256,256]{2,1,0:T(8,128)(2,1)}), bf16[4,256,256]{2,1,0:T(8,128)(2,1)S(1)}, u32[]{:S(2)}, u32[]{:S(2)}) %all-to-all-start.1) | async-done | bytes 524320 | tf_op jit(solution)/shard_map/all_to_all | solution.py:145
  45.9 2.5 multiply_reduce_fusion
  48.6 0.9 reshape.360
  49.5 11.8 %all-to-all-start.2 = ((bf16[32,2,1024]{2,1,0:T(2,128)(2,1)}), bf16[32,2,1024]{2,1,0:T(2,128)(2,1)S(1)}, u32[]{:S(2)}, u32[]{:S(2)}) async-start(bf16[32,2,1024]{2,1,0:T(2,128)(2,1)} %reshape.360), calls=%async_computation.3 | async-start | bytes 262144 | tf_op jit(solution)/shard_map/all_to_all | solution.py:46
  61.4 5.7 %multiply_reduce_fusion.1 = bf16[1024,128]{1,0:T(8,128)(2,1)S(1)} fusion(bf16[1024,2,128]{2,1,0:T(2,128)(2,1)S(1)} %reshape_reshape.3, bf16[1024,2]{1,0:T(8,128)(2,1)S(1)} %copy.41), kind=kLoop, calls=%fused_computation.18 | loop fusion | flops 393216 | bytes 790528 | tf_op jit(solution)/shard_map/reduce_sum | solution.py:87
  67.1 2.3 fusion.4
  69.5 17.7 %fusion = f32[1024,1,128]{2,1,0:T(1,128)S(1)} fusion(pred[1024,32,1]{1,2,0:T(4,128)(4,1)S(1)} %copy-done.5, bf16[1024,32,128]{2,0,1:T(8,128)(2,1)S(1)} %fusion.4), kind=kOutput, calls=%fused_computation.3 | convolution fusion | flops 8388608 | bytes 8945664 | tf_op jit(solution)/shard_map/svj,sv->sj/dot_general | solution.py:92
  87.5 0.8 reshape.362
  88.4 9.4 %all-to-all-start.3 = ((bf16[32,2,1024]{2,1,0:T(2,128)(2,1)}), bf16[32,2,1024]{2,1,0:T(2,128)(2,1)S(1)}, u32[]{:S(2)}, u32[]{:S(2)}) async-start(bf16[32,2,1024]{2,1,0:T(2,128)(2,1)} %reshape.362), calls=%async_computation.4 | async-start | bytes 262144 | tf_op jit(solution)/shard_map/all_to_all | solution.py:25
  97.8 3.9 %broadcast_multiply_fusion.1 = f32[1024,2,128]{2,1,0:T(2,128)S(1)} fusion(f32[1024,128]{1,0:T(8,128)S(1)} %bitcast.75, f32[1024,2]{1,0:T(8,128)S(1)} %copy-done.3), kind=kLoop, calls=%fused_computation.17 | loop fusion | flops 262144 | bytes 1581056 | tf_op jit(solution)/shard_map/mul | solution.py:93
  101.7 6.3 %all-to-all-done.3 = bf16[32,2,1024]{2,1,0:T(2,128)(2,1)S(1)} async-done(((bf16[32,2,1024]{2,1,0:T(2,128)(2,1)}), bf16[32,2,1024]{2,1,0:T(2,128)(2,1)S(1)}, u32[]{:S(2)}, u32[]{:S(2)}) %all-to-all-start.3) | async-done | bytes 131104 | tf_op jit(solution)/shard_map/all_to_all | solution.py:25
  108.4 1.1 broadcast_multiply_fusion
  109.5 2.2 fusion.3
  111.7 3.5 %all-to-all-start.4 = ((bf16[4,256,256]{2,1,0:T(8,128)(2,1)}), bf16[4,256,256]{2,1,0:T(8,128)(2,1)S(1)}, u32[]{:S(2)}, u32[]{:S(2)}) async-start(bf16[4,256,256]{2,1,0:T(8,128)(2,1)} %bitcast.24), calls=%async_computation.5 | async-start | bytes 1048576 | tf_op jit(solution)/shard_map/all_to_all | solution.py:165
  115.5 6.6 %all-to-all-done.4 = bf16[4,256,256]{2,1,0:T(8,128)(2,1)S(1)} async-done(((bf16[4,256,256]{2,1,0:T(8,128)(2,1)}), bf16[4,256,256]{2,1,0:T(8,128)(2,1)S(1)}, u32[]{:S(2)}, u32[]{:S(2)}) %all-to-all-start.4) | async-done | bytes 524320 | tf_op jit(solution)/shard_map/all_to_all | solution.py:165
  122.1 1.9 gather_fusion.2
  124.2 122.6 %reduce-scatter.2.cloned.1.call-done = bf16[256,512]{1,0:T(8,128)(2,1)} async-done(((bf16[8192,512]{1,0:T(8,128)(2,1)}), bf16[256,512]{1,0:T(8,128)(2,1)}) %reduce-scatter.2.cloned.1.call-update) | async-done | bytes 262160 | tf_op jit(solution)/shard_map/reduce_scatter | solution.py:12
  246.8 1.1 add_convert_fusion.1
  247.9 1.3 collective-permute-start
  249.2 5.7 %collective-permute-done = bf16[512,256]{0,1:T(8,128)(2,1)S(1)} collective-permute-done((bf16[512,256]{0,1:T(8,128)(2,1)S(1)}, bf16[512,256]{0,1:T(8,128)(2,1)S(1)}, u32[]{:S(2)}, u32[]{:S(2)}) %collective-permute-start) | collective-permute-done | bytes 262176 | tf_op jit(solution)/shard_map/ppermute | solution.py:60
  254.9 1.1 fusion.7
  256.0 0.8 copy.45
  (52 shorter events, 4.4 us)
Async XLA Ops:
  6.5 103.0 %copy-start = (bf16[1,32,64,256]{3,2,1,0:T(8,128)(2,1)S(1)}, bf16[1,32,64,256]{3,2,1,0:T(8,128)(2,1)}, u32[]{:S(2)}) copy-start(bf16[1,32,64,256]{3,2,1,0:T(8,128)(2,1)} %param.12) | copy-start | bytes 3145732
  6.5 8.0 %copy-start.1 = (s32[512]{0:T(512)S(1)}, s32[512]{0:T(512)}, u32[]{:S(2)}) copy-start(s32[512]{0:T(512)} %param.15) | copy-start | bytes 6148
  6.5 240.2 %reduce-scatter.2.cloned.1.call-start = ((), (), s32[]{:S(2)}) async-start(), calls=%async_computation.6 | async-start | bytes 8650752 | tf_op jit(solution)/shard_map/reduce_scatter | solution.py:12
  14.5 14.0 %copy-start.2 = (bf16[1,512,256]{2,1,0:T(8,128)(2,1)S(1)}, bf16[1,512,256]{2,1,0:T(8,128)(2,1)}, u32[]{:S(2)}) copy-start(bf16[1,512,256]{2,1,0:T(8,128)(2,1)} %param.9) | copy-start | bytes 786436
  14.5 18.0 %copy-start.7 = (s32[1,32,1]{1,2,0:T(1,128)S(1)}, s32[1,32,1]{1,2,0:T(1,128)}, u32[]{:S(2)}) copy-start(s32[1,32,1]{1,2,0:T(1,128)} %param.14) | copy-start | bytes 388
  14.5 19.3 %copy-start.4 = (bf16[1,32,1,128,128]{4,3,2,1,0:T(8,128)(2,1)S(1)}, bf16[1,32,1,128,128]{4,3,2,1,0:T(8,128)(2,1)}, u32[]{:S(2)}) copy-start(bf16[1,32,1,128,128]{4,3,2,1,0:T(8,128)(2,1)} %param.13) | copy-start | bytes 3145732
  23.7 10.8 %all-to-all-start = ((bf16[4,2,128]{2,1,0:T(2,128)(2,1)}), bf16[4,2,128]{2,1,0:T(2,128)(2,1)S(1)}, u32[]{:S(2)}, u32[]{:S(2)}) async-start(bf16[4,2,128]{2,1,0:T(2,128)(2,1)} %reshape.358), calls=%async_computation.1 | async-start | bytes 4096 | tf_op jit(solution)/shard_map/all_to_all | solution.py:146
  34.5 11.4 %all-to-all-start.1 = ((bf16[4,256,256]{2,1,0:T(8,128)(2,1)}), bf16[4,256,256]{2,1,0:T(8,128)(2,1)S(1)}, u32[]{:S(2)}, u32[]{:S(2)}) async-start(bf16[4,256,256]{2,1,0:T(8,128)(2,1)} %select_select_fusion), calls=%async_computation.2 | async-start | bytes 1048576 | tf_op jit(solution)/shard_map/all_to_all | solution.py:145
  49.5 37.7 %all-to-all-start.2 = ((bf16[32,2,1024]{2,1,0:T(2,128)(2,1)}), bf16[32,2,1024]{2,1,0:T(2,128)(2,1)S(1)}, u32[]{:S(2)}, u32[]{:S(2)}) async-start(bf16[32,2,1024]{2,1,0:T(2,128)(2,1)} %reshape.360), calls=%async_computation.3 | async-start | bytes 262144 | tf_op jit(solution)/shard_map/all_to_all | solution.py:46
  67.1 2.4 copy-start.5
  69.5 28.4 %copy-start.3 = (f32[1024,2]{1,0:T(8,128)S(1)}, f32[1024,2]{1,0:T(8,128)}, u32[]{:S(2)}) copy-start(f32[1024,2]{1,0:T(8,128)} %copy.40) | copy-start | bytes 24580
  88.4 19.6 %all-to-all-start.3 = ((bf16[32,2,1024]{2,1,0:T(2,128)(2,1)}), bf16[32,2,1024]{2,1,0:T(2,128)(2,1)S(1)}, u32[]{:S(2)}, u32[]{:S(2)}) async-start(bf16[32,2,1024]{2,1,0:T(2,128)(2,1)} %reshape.362), calls=%async_computation.4 | async-start | bytes 262144 | tf_op jit(solution)/shard_map/all_to_all | solution.py:25
  108.3 7.0 %copy-start.6 = (bf16[512,256]{1,0:T(8,128)(2,1)S(1)}, bf16[512,256]{1,0:T(8,128)(2,1)}, u32[]{:S(2)}) copy-start(bf16[512,256]{1,0:T(8,128)(2,1)} %param.8) | copy-start | bytes 786436
  111.7 10.4 %all-to-all-start.4 = ((bf16[4,256,256]{2,1,0:T(8,128)(2,1)}), bf16[4,256,256]{2,1,0:T(8,128)(2,1)S(1)}, u32[]{:S(2)}, u32[]{:S(2)}) async-start(bf16[4,256,256]{2,1,0:T(8,128)(2,1)} %bitcast.24), calls=%async_computation.5 | async-start | bytes 1048576 | tf_op jit(solution)/shard_map/all_to_all | solution.py:165
  247.9 7.0 %collective-permute-start = (bf16[512,256]{0,1:T(8,128)(2,1)S(1)}, bf16[512,256]{0,1:T(8,128)(2,1)S(1)}, u32[]{:S(2)}, u32[]{:S(2)}) collective-permute-start(bf16[512,256]{0,1:T(8,128)(2,1)S(1)} %add_convert_fusion.1), channel_id=1, source_target_pairs={{0,32},{1,33},{2,34},{3,35},{4,36},{5,37},{6,38},{7,39},{8,40},{9,... | collective-permute-start | bytes 786440 | tf_op jit(solution)/shard_map/ppermute | solution.py:60
Sparse Core Ops, SparseCore 0:
  14.6 232.1 reduce-scatter.1
